TPU v7x, 32 devices: a whole 2x2x4 slice. The times are simulated.
32 devices in a mesh: dp: 8 (over y, x, core), tensor: 4 (over z).
Axes of the slice: x: 2, y: 2, z: 4, core: 2. Of those that a mesh axis runs over, the one named last changes fastest.
Arguments:
- tokens: bfloat16 [4096, 2048], P('dp'), may hold values from -6 to 6
- seq_ids: int32 [4096], replicated, may hold values from 0 to 3, never falling along the last dimension, each value on 1 to 2048 neighbouring positions
- route_ids: int32 [4096, 6], P('dp'), may hold values from 0 to 63, all different within a row; in each aligned block of 512 rows (0 to 511, 512 to 1023, ...) at most 72 rows name the same one
- cotangent: bfloat16 [4096, 2048], P('dp'), may hold values from -6 to 6
- input_gain: float32 [2048], replicated, may hold values from 0.5 to 1.5
- w_query: bfloat16 [2048, 3072], P(None, 'tensor'), may hold values from -0.125 to 0.125
- w_latent: bfloat16 [2048, 576], replicated, may hold values from -0.125 to 0.125
- latent_gain: float32 [512], replicated, may hold values from 0.5 to 1.5
- w_expand: bfloat16 [512, 4096], P(None, 'tensor'), may hold values from -0.25 to 0.25
- w_out: bfloat16 [2048, 2048], P('tensor'), may hold values from -0.5 to 0.5
- middle_gain: float32 [2048], replicated, may hold values from 0.5 to 1.5
- w_router: bfloat16 [2048, 64], replicated, may hold values from -0.0390625 to 0.0390625
- expert_gate: bfloat16 [64, 2048, 1408], P('dp', None, 'tensor'), may hold values from -0.125 to 0.125
- expert_up: bfloat16 [64, 2048, 1408], P('dp', None, 'tensor'), may hold values from -0.125 to 0.125
- expert_down: bfloat16 [64, 1408, 2048], P('dp', 'tensor'), may hold values from -2.5 to 2.5
- shared_gate: bfloat16 [2048, 2816], P(None, 'tensor'), may hold values from -0.125 to 0.125
- shared_up: bfloat16 [2048, 2816], P(None, 'tensor'), may hold values from -0.125 to 0.125
- shared_down: bfloat16 [2816, 2048], P('tensor'), may hold values from -0.21875 to 0.21875
Outputs:
- output: bfloat16 [4096, 2048], P('dp')
- token_grad: bfloat16 [4096, 2048], P('dp')
- grad_input_gain: float32 [2048], P('dp')
- grad_query: float32 [2048, 3072], P('dp', 'tensor')
- grad_latent: float32 [2048, 576], P('dp')
- grad_latent_gain: float32 [512], P('dp')
- grad_expand: float32 [512, 4096], P('dp', 'tensor')
- grad_out_proj: float32 [2048, 2048], P('tensor', 'dp')
- grad_middle_gain: float32 [2048], P('dp')
- grad_router: float32 [2048, 64], P('dp')
- grad_expert_gate: float32 [64, 2048, 1408], P('dp', None, 'tensor')
- grad_expert_up: float32 [64, 2048, 1408], P('dp', None, 'tensor')
- grad_expert_down: float32 [64, 1408, 2048], P('dp', 'tensor')
- grad_shared_gate: float32 [2048, 2816], P('dp', 'tensor')
- grad_shared_up: float32 [2048, 2816], P('dp', 'tensor')
- grad_shared_down: float32 [2816, 2048], P('tensor', 'dp')
Inputs may be any that keep to these rules, and one draw needn't show every extreme that they name: seq_ids never fall; each sequence has 1 to 2048 tokens, one has exactly 2048. `route_ids`: each row names 6 different experts; in the rows of one data block (512 tokens) no expert is named by more than 72 rows, a bound that some block reaches.
All inputs are finite; a program needn't handle non-finite values.
Results may differ from a plain program's by a relative error of at most 0.025.
Values may be sent and summed in bfloat16 or wider, within the bound.
No kernel may reach another device: no remote copies, remote signals or barrier semaphores. Data moves between devices by JAX's collectives and lax.ppermute only.
A program may use at most 448 MiB of HBM per device.

v0:
```python
import jax
import jax.numpy as jnp
from jax import lax
from jax.sharding import PartitionSpec as P

DN = 128
DR = 64
DV = 128
KVR = 512
REACH = 4
CAP = 72
BF = jnp.bfloat16
F32 = jnp.float32
epsilon = 1e-06


def dot(eq, a, b):
    return jnp.einsum(eq, a, b, preferred_element_type=F32)


def passed_along(shard, axis, by):
    peers = lax.axis_size(axis)
    pairs = [(i, i + by) for i in range(peers) if 0 <= i + by < peers]
    return lax.ppermute(shard, axis, pairs)


def normed(values, norm_gain):
    return (
        values * lax.rsqrt(jnp.mean(values * values, axis=-1, keepdims=True) + epsilon) * norm_gain
    )


def norm_backward(values, norm_gain, upstream):
    _, pullback = jax.vjp(normed, values, norm_gain)
    return pullback(upstream)


def rotate(values, cosine, sine):
    half = values.shape[-1] // 2
    front, back = (values[..., :half], values[..., half:])
    return jnp.concatenate([front * cosine - back * sine, back * cosine + front * sine], axis=-1)


def rotate_back(upstream, cosine, sine):
    return rotate(upstream, cosine, -sine)


def silu_gate(gate_val, up_val):
    return gate_val * jax.nn.sigmoid(gate_val) * up_val


def silu_backward(gate_val, up_val, upstream):
    _, pullback = jax.vjp(silu_gate, gate_val, up_val)
    return pullback(upstream)


def rope_tables(seq_all, seq_here, index_here):
    starts = jnp.sum((seq_all[None, :] < seq_here[:, None]).astype(jnp.int32), axis=1)
    position = (index_here - starts).astype(F32)
    frequency = 10000.0 ** (-(jnp.arange(DR // 2, dtype=F32) * 2.0) / DR)
    angle = position[:, None] * frequency[None, :]
    return (jnp.cos(angle), jnp.sin(angle))


def scatter_sum(parts):
    joined = jnp.concatenate(parts, axis=1)
    summed = lax.psum_scatter(joined, "dp", scatter_dimension=0, tiled=True)
    out, at = ([], 0)
    for part in parts:
        out.append(summed[:, at : at + part.shape[1]].astype(F32))
        at += part.shape[1]
    return out


def shards(
    tokens,
    seq_ids,
    route_ids,
    cotangent,
    input_gain,
    w_query,
    w_latent,
    latent_gain,
    w_expand,
    w_out,
    middle_gain,
    w_router,
    expert_gate,
    expert_up,
    expert_down,
    shared_gate,
    shared_up,
    shared_down,
):
    devices = lax.axis_size("dp")
    rank_dp = lax.axis_index("dp")
    tok_rows, width = tokens.shape
    experts_local = expert_gate.shape[0]
    heads_local = w_query.shape[1] // (DN + DR)
    reach = min(REACH, devices - 1)
    window = (reach + 1) * tok_rows
    scale = (DN + DR) ** (-0.5)
    cot_all = lax.all_gather(cotangent, "dp", tiled=True)
    route_all = lax.all_gather(route_ids, "dp", tiled=True)
    index_here = rank_dp * tok_rows + jnp.arange(tok_rows, dtype=jnp.int32)
    seq_here = lax.dynamic_slice_in_dim(seq_ids, rank_dp * tok_rows, tok_rows, 0)
    cosine, sine = rope_tables(seq_ids, seq_here, index_here)
    key_index = (rank_dp - reach) * tok_rows + jnp.arange(window, dtype=jnp.int32)
    seq_padded = jnp.concatenate([jnp.full((reach * tok_rows,), -1, jnp.int32), seq_ids])
    seq_keys = lax.dynamic_slice_in_dim(seq_padded, rank_dp * tok_rows, window, 0)
    allowed = (seq_here[:, None] == seq_keys[None, :]) & (key_index[None, :] <= index_here[:, None])
    token_features = tokens.astype(F32)
    grad_output = cotangent.astype(F32)
    hidden_in = normed(token_features, input_gain).astype(BF)
    latent_full = jnp.dot(hidden_in, w_latent, preferred_element_type=F32)
    latent_raw = latent_full[:, :KVR]
    latent = normed(latent_raw, latent_gain).astype(BF)
    rope_key = rotate(latent_full[:, KVR:], cosine, sine).astype(BF)
    own_keys = jnp.concatenate([latent, rope_key], axis=1)
    earlier = [passed_along(own_keys, "dp", back) for back in range(reach, 0, -1)]
    keys_window = jnp.concatenate(earlier + [own_keys], axis=0)
    latent_window = keys_window[:, :KVR]
    rope_window = keys_window[:, KVR:]
    query_pre = jnp.dot(hidden_in, w_query, preferred_element_type=F32).reshape(
        tok_rows, heads_local, DN + DR
    )
    queries = jnp.concatenate(
        [query_pre[..., :DN], rotate(query_pre[..., DN:], cosine[:, None, :], sine[:, None, :])],
        axis=-1,
    ).astype(BF)
    expanded = (
        jnp.dot(latent_window, w_expand, preferred_element_type=F32)
        .astype(BF)
        .reshape(window, heads_local, DN + DV)
    )
    key_nope = expanded[..., :DN]
    key_value = expanded[..., DN:]
    scores = dot("qhd,khd->hqk", queries[..., :DN], key_nope) + dot(
        "qhd,kd->hqk", queries[..., DN:], rope_window
    )
    scores = jnp.where(allowed[None], scores * scale, -1e30)
    probs = jax.nn.softmax(scores, axis=-1)
    probs_low = probs.astype(BF)
    attended = (
        dot("hqk,khd->qhd", probs_low, key_value).astype(BF).reshape(tok_rows, heads_local * DV)
    )
    attention = lax.psum(
        jnp.dot(attended, w_out, preferred_element_type=F32).astype(BF), "tensor"
    ).astype(F32)
    middle = token_features + attention
    hidden_mid = normed(middle, middle_gain).astype(BF)
    hidden_all = lax.all_gather(hidden_mid, "dp", tiled=True)
    shared_gate_val = jnp.dot(hidden_mid, shared_gate, preferred_element_type=F32)
    shared_up_val = jnp.dot(hidden_mid, shared_up, preferred_element_type=F32)
    shared_active = silu_gate(shared_gate_val, shared_up_val).astype(BF)
    shared_result = jnp.dot(shared_active, shared_down, preferred_element_type=F32)
    shared_active_grad = dot("td,fd->tf", cotangent, shared_down)
    shared_gate_grad, shared_up_grad = silu_backward(
        shared_gate_val, shared_up_val, shared_active_grad
    )
    shared_gate_grad = shared_gate_grad.astype(BF)
    shared_up_grad = shared_up_grad.astype(BF)
    mid_from_shared = dot("tf,df->td", shared_gate_grad, shared_gate) + dot(
        "tf,df->td", shared_up_grad, shared_up
    )
    grad_shared_down = dot("td,tf->df", cotangent, shared_active).astype(BF)
    grad_shared_gate = dot("td,tf->df", hidden_mid, shared_gate_grad).astype(BF)
    grad_shared_up = dot("td,tf->df", hidden_mid, shared_up_grad).astype(BF)
    local_ids = rank_dp * experts_local + jnp.arange(experts_local, dtype=jnp.int32)
    named = jnp.any(route_all[:, :, None] == local_ids[None, None, :], axis=1)
    named_block = named.reshape(devices, tok_rows, experts_local)
    before = jnp.tril(jnp.ones((tok_rows, tok_rows), BF), -1)
    rank_within = dot("ts,bse->bet", before, named_block.astype(BF)).astype(jnp.int32)
    slot = jnp.where(named_block.transpose(0, 2, 1), rank_within, -1)
    chosen = (slot[:, :, None, :] == jnp.arange(CAP, dtype=jnp.int32)[None, None, :, None]).astype(
        BF
    )
    logits = jnp.dot(hidden_all, w_router, preferred_element_type=F32)
    router_probs = jax.nn.softmax(logits, axis=-1)
    local_probs = lax.dynamic_slice_in_dim(
        router_probs, rank_dp * experts_local, experts_local, 1
    ).reshape(devices, tok_rows, experts_local)
    slot_gates = jnp.sum(
        chosen.astype(F32) * local_probs.transpose(0, 2, 1)[:, :, None, :], axis=-1
    )
    cot_rows = dot("bect,btd->becd", chosen, cot_all.reshape(devices, tok_rows, width)).astype(BF)
    rows = dot("bect,btd->becd", chosen, hidden_all.reshape(devices, tok_rows, width)).astype(BF)
    gate_val = dot("becd,edf->becf", rows, expert_gate)
    up_val = dot("becd,edf->becf", rows, expert_up)
    down_back = dot("becd,efd->becf", cot_rows, expert_down)
    active = silu_gate(gate_val, up_val).astype(BF)
    gated_active = active.astype(F32) * slot_gates[..., None]
    gate_grad = jnp.sum(active.astype(F32) * down_back, axis=-1)
    gate_val_grad, up_val_grad = silu_backward(gate_val, up_val, down_back * slot_gates[..., None])
    gate_val_grad = gate_val_grad.astype(BF)
    up_val_grad = up_val_grad.astype(BF)
    gated_active = gated_active.astype(BF)
    row_grad = (
        dot("becf,edf->becd", gate_val_grad, expert_gate)
        + dot("becf,edf->becd", up_val_grad, expert_up)
    ).astype(BF)
    row_out = dot("becf,efd->becd", gated_active, expert_down).astype(BF)
    probs_grad = dot("bect,bec->bte", chosen, gate_grad.astype(BF)).reshape(-1, experts_local)
    probs_grad = lax.dynamic_update_slice_in_dim(
        jnp.zeros_like(router_probs), probs_grad, rank_dp * experts_local, 1
    )
    logit_grad = (
        router_probs * (probs_grad - jnp.sum(router_probs * probs_grad, axis=-1, keepdims=True))
    ).astype(BF)
    grad_router = dot("td,te->de", hidden_all, logit_grad)
    mid_part = dot("bect,becd->btd", chosen, row_grad).reshape(-1, width) + dot(
        "te,de->td", logit_grad, w_router
    )
    mid_block = lax.psum_scatter(mid_part.astype(BF), "dp", scatter_dimension=0, tiled=True)
    mid_grad = lax.psum((mid_block.astype(F32) + mid_from_shared).astype(BF), "tensor").astype(F32)
    routed_part = dot("bect,becd->btd", chosen, row_out).reshape(-1, width).astype(BF)
    routed_part, _ = lax.optimization_barrier((routed_part, mid_block))
    routed_block = lax.psum_scatter(routed_part, "dp", scatter_dimension=0, tiled=True)
    grad_expert_down = dot("becf,becd->efd", gated_active, cot_rows)
    grad_expert_gate = dot("becd,becf->edf", rows, gate_val_grad)
    grad_expert_up = dot("becd,becf->edf", rows, up_val_grad)
    middle_from_norm, grad_middle_gain = norm_backward(middle, middle_gain, mid_grad)
    middle_grad = grad_output + middle_from_norm
    middle_low = middle_grad.astype(BF)
    grad_out_proj = dot("td,tc->dc", middle_low, attended).astype(BF)
    attended_grad = (
        dot("td,cd->tc", middle_low, w_out).astype(BF).reshape(tok_rows, heads_local, DV)
    )
    probs_grad_att = dot("qhd,khd->hqk", attended_grad, key_value)
    score_grad = (
        probs * (probs_grad_att - jnp.sum(probs * probs_grad_att, axis=-1, keepdims=True))
    ).astype(BF)
    query_nope_grad = dot("hqk,khd->qhd", score_grad, key_nope) * scale
    query_rope_grad = dot("hqk,kd->qhd", score_grad, rope_window) * scale
    key_nope_grad = dot("hqk,qhd->khd", score_grad, queries[..., :DN]) * scale
    rope_window_grad = dot("hqk,qhd->kd", score_grad, queries[..., DN:]) * scale
    value_grad = dot("hqk,qhd->khd", probs_low, attended_grad)
    expanded_grad = (
        jnp.concatenate([key_nope_grad, value_grad], axis=-1)
        .astype(BF)
        .reshape(window, heads_local * (DN + DV))
    )
    latent_window_grad = dot("wc,kc->wk", expanded_grad, w_expand)
    grad_expand = dot("wk,wc->kc", latent_window, expanded_grad).astype(BF)
    window_grad = jnp.concatenate([latent_window_grad, rope_window_grad], axis=1)
    keys_grad = window_grad[reach * tok_rows :]
    for back in range(reach, 0, -1):
        start = (reach - back) * tok_rows
        piece = window_grad[start : start + tok_rows].astype(BF)
        keys_grad = keys_grad + passed_along(piece, "dp", -back).astype(F32)
    query_grad = (
        jnp.concatenate(
            [query_nope_grad, rotate_back(query_rope_grad, cosine[:, None, :], sine[:, None, :])],
            axis=-1,
        )
        .astype(BF)
        .reshape(tok_rows, heads_local * (DN + DR))
    )
    grad_query = dot("td,tc->dc", hidden_in, query_grad).astype(BF)
    input_from_query = dot("tc,dc->td", query_grad, w_query)
    keys_grad = lax.psum(keys_grad.astype(BF), "tensor").astype(F32)
    latent_raw_grad, grad_latent_gain = norm_backward(latent_raw, latent_gain, keys_grad[:, :KVR])
    rope_raw_grad = rotate_back(keys_grad[:, KVR:], cosine, sine)
    latent_full_grad = jnp.concatenate([latent_raw_grad, rope_raw_grad], axis=-1).astype(BF)
    grad_latent = dot("td,tc->dc", hidden_in, latent_full_grad).astype(BF)
    input_grad = lax.psum(input_from_query.astype(BF), "tensor").astype(F32) + dot(
        "tc,dc->td", latent_full_grad, w_latent
    )
    token_from_norm, grad_input_gain = norm_backward(token_features, input_gain, input_grad)
    token_grad = (middle_grad + token_from_norm).astype(BF)
    routed_block, _ = lax.optimization_barrier((routed_block, mid_grad))
    feedforward = lax.psum((routed_block.astype(F32) + shared_result).astype(BF), "tensor")
    output = (middle + feedforward.astype(F32)).astype(BF)
    grad_shared_down, grad_shared_gate, grad_shared_up = scatter_sum(
        [grad_shared_down, grad_shared_gate, grad_shared_up]
    )
    grad_router = lax.psum(grad_router.astype(BF), "tensor")
    gains = jnp.stack(
        [grad_middle_gain, grad_input_gain, jnp.repeat(grad_latent_gain, width // KVR)], axis=1
    ).astype(BF)
    grad_out_proj, grad_query, grad_latent, grad_expand, grad_router, gains = scatter_sum(
        [grad_out_proj, grad_query, grad_latent, grad_expand.reshape(width, -1), grad_router, gains]
    )
    grad_expand = grad_expand.reshape(KVR // devices, -1)
    return (
        output,
        token_grad,
        gains[:, 1],
        grad_query,
        grad_latent,
        gains[:: width // KVR, 2],
        grad_expand,
        grad_out_proj.T,
        gains[:, 0],
        grad_router,
        grad_expert_gate,
        grad_expert_up,
        grad_expert_down,
        grad_shared_gate,
        grad_shared_up,
        grad_shared_down.T,
    )


def solution(mesh):
    placed = (
        P("dp", None),
        P(),
        P("dp", None),
        P("dp", None),
        P(),
        P(None, "tensor"),
        P(),
        P(),
        P(None, "tensor"),
        P("tensor", None),
        P(),
        P(),
        P("dp", None, "tensor"),
        P("dp", None, "tensor"),
        P("dp", "tensor", None),
        P(None, "tensor"),
        P(None, "tensor"),
        P("tensor", None),
    )
    return jax.shard_map(
        shards,
        mesh=mesh,
        in_specs=placed,
        out_specs=(
            P("dp", None),
            P("dp", None),
            P("dp"),
            P("dp", "tensor"),
            P("dp", None),
            P("dp"),
            P("dp", "tensor"),
            P("tensor", "dp"),
            P("dp"),
            P("dp", None),
            P("dp", None, "tensor"),
            P("dp", None, "tensor"),
            P("dp", "tensor", None),
            P("dp", "tensor"),
            P("dp", "tensor"),
            P("tensor", "dp"),
        ),
        check_vma=False,
    )
```

profile of v0, /device:TPU:0, one launch (start us, length us, event | category | flops | bytes accessed | tf_op | source)
XLA Modules:
  0.0 1195.1 jit_solution(14079437632044810351)
XLA Ops:
  40.0 25.1 %collective-permute-done = bf16[512,576]{0,1:T(8,128)(2,1)} collective-permute-done((bf16[512,576]{0,1:T(8,128)(2,1)}, bf16[512,576]{0,1:T(8,128)(2,1)}, u32[]{:S(2)}, u32[]{:S(2)}) %collective-permute-start) | collective-permute-done | bytes 589856 | tf_op jit(solution)/shard_map/ppermute | solution.py:24
  73.0 8.9 fusion.82
  82.0 13.6 %fusion.3 = f32[4,512,2560]{2,1,0:T(8,128)} fusion(f32[4,512,2560]{2,1,0:T(8,128)} %fusion.82, pred[512,2560]{1,0:T(8,128)(4,1)S(1)} %compare_and_fusion, bf16[2560,576]{0,1:T(8,128)(2,1)} %copy-done.37, bf16[512,4,32]{0,2,1:T(8,128)(2,1)S(1)} %get-tuple-element.126, bf16[512,4,32]{0,2,1:T(8,128)(2,1)S(1)} %get-tuple-element.125), kind=kOutput, calls=%fused_computation.7 | convolution fusion | flops 687341568 | bytes 43843584 | tf_op jit(solution)/shard_map/qhd,kd->hqk/dot_general | solution.py:18
  95.6 23.5 %fusion.169 = (f32[4,512]{1,0:T(4,128)S(1)}, f32[4,512,2560]{2,1,0:T(8,128)}) fusion(f32[4,512,2560]{2,1,0:T(8,128)} %fusion.3), kind=kOutput, calls=%fused_computation.251 | output fusion | flops 10488319 | bytes 41951232 | tf_op jit(solution)/shard_map/sub | solution.py:142
  119.1 17.4 %fusion.105 = bf16[4,128,512]{2,1,0:T(8,128)(2,1)} fusion(bf16[2560,4,256]{0,2,1:T(8,128)(2,1)} %bitcast.238, f32[4,512]{1,0:T(4,128)S(1)} %get-tuple-element.144, f32[4,512,2560]{2,1,0:T(8,128)} %fusion.3), kind=kOutput, calls=%fused_computation.147 | convolution fusion | flops 1358172672 | bytes 45096960 | tf_op jit(solution)/shard_map/hqk,khd->qhd/dot_general | solution.py:18
  141.5 91.4 %all-reduce.6.cloned.1.call-done = bf16[512,2048]{1,0:T(8,128)(2,1)} async-done(((bf16[512,2048]{1,0:T(8,128)(2,1)}), bf16[512,2048]{1,0:T(8,128)(2,1)}) %all-reduce.6.cloned.1.call-update) | async-done | bytes 2097168 | tf_op jit(solution)/shard_map/psum | solution.py:147
  239.6 9.4 all_gather.9
  252.7 18.8 %convolution_convert_fusion = bf16[8,8,72,2048]{3,2,1,0:T(8,128)(2,1)} fusion(bf16[8,512,2048,1]{2,1,3,0:T(8,128)(2,1)} %bitcast.249, s32[8,8,512]{2,1,0:T(8,128)S(1)} %fusion.120), kind=kOutput, calls=%fused_computation.26 | convolution fusion | flops 9675472896 | bytes 35782656 | tf_op jit(solution)/shard_map/bect,btd->becd/dot_general | solution.py:18
  271.4 59.2 %all-gather.3.cloned.1.call-done = bf16[4096,2048]{1,0:T(8,128)(2,1)} async-done(((bf16[512,2048]{1,0:T(8,128)(2,1)}), bf16[4096,2048]{1,0:T(8,128)(2,1)}) %all-gather.3.cloned.1.call-update) | async-done | bytes 16777232 | tf_op jit(solution)/shard_map/all_gather | solution.py:152
  330.6 18.8 %convolution_convert_fusion.1 = bf16[8,8,72,2048]{3,2,1,0:T(8,128)(2,1)} fusion(bf16[8,512,2048,1]{2,1,3,0:T(8,128)(2,1)} %bitcast.222, s32[8,8,512]{2,1,0:T(8,128)S(1)} %fusion.120), kind=kOutput, calls=%fused_computation.27 | convolution fusion | flops 9675472896 | bytes 35782656 | tf_op jit(solution)/shard_map/bect,btd->becd/dot_general | solution.py:18
  349.4 20.0 %fusion.18 = f32[8,8,72,352]{3,2,1,0:T(8,128)} fusion(bf16[8,8,72,2048]{3,2,1,0:T(8,128)(2,1)} %convolution_convert_fusion.1, bf16[8,2048,352]{1,2,0:T(8,128)(2,1)} %param.31), kind=kOutput, calls=%fused_computation.22 | convolution fusion | flops 6643777536 | bytes 36896768 | tf_op jit(solution)/shard_map/becd,edf->becf/dot_general | solution.py:18
  369.4 20.4 %fusion.20 = f32[8,8,72,352]{3,2,1,0:T(8,128)} fusion(bf16[8,8,72,2048]{3,2,1,0:T(8,128)(2,1)} %convolution_convert_fusion.1, bf16[8,2048,352]{1,2,0:T(8,128)(2,1)} %param.30), kind=kOutput, calls=%fused_computation.24 | convolution fusion | flops 6643777536 | bytes 36896768 | tf_op jit(solution)/shard_map/becd,edf->becf/dot_general | solution.py:18
  389.9 24.2 %fusion.39 = (bf16[8,8,72]{2,0,1:T(8,128)(2,1)S(1)}, bf16[8,8,72,352]{3,2,0,1:T(8,128)(2,1)}, f32[8,8,72,352]{3,2,1,0:T(8,128)}) fusion(f32[8,8,72,352]{3,2,1,0:T(8,128)} %fusion.18, f32[8,8,72,352]{3,2,1,0:T(8,128)} %fusion.20, bf16[8,352,2048]{2,1,0:T(8,128)(2,1)} %param.32, bf16[8,8,72,2048]{3,2,1,0:T(8,128)(2,1)} %convolution_convert_fusion), kind=kOutput, calls=%fused_computation.56 | convolution fusion | flops 6658371072 | bytes 53126144 | tf_op jit(solution)/shard_map/becd,efd->becf/dot_general | solution.py:18
  415.7 11.1 fusion.170
  436.6 21.0 %fusion.31 = f32[8,8,72,2048]{3,2,0,1:T(8,128)} fusion(bf16[8,2048,352]{1,2,0:T(8,128)(2,1)} %param.30, bf16[8,8,72,352]{3,2,0,1:T(8,128)(2,1)} %get-tuple-element.115), kind=kOutput, calls=%fused_computation.33 | convolution fusion | flops 6643777536 | bytes 52527104 | tf_op jit(solution)/shard_map/becf,edf->becd/dot_general | solution.py:18
  457.6 40.2 %fusion.5 = f32[8,512,2048,1]{2,1,3,0:T(8,128)} fusion(f32[8,8,72,2048]{3,2,0,1:T(8,128)} %fusion.31, bf16[8,2048,352]{1,2,0:T(8,128)(2,1)} %param.31, bf16[8,8,72,352]{3,2,0,1:T(8,128)(2,1)} %get-tuple-element.114, pred[8,8,72,512]{3,2,1,0:T(8,128)(4,1)} %iota_compare_fusion.14), kind=kOutput, calls=%fused_computation.12 | convolution fusion | flops 16326328320 | bytes 88440832 | tf_op jit(solution)/shard_map/bect,becd->btd/dot_general | solution.py:18
  497.8 17.1 %fusion.1 = bf16[4096,2048]{1,0:T(8,128)(2,1)} fusion(f32[8,512,2048,1]{2,1,3,0:T(8,128)} %fusion.5, bf16[4096,64]{0,1:T(8,128)(2,1)} %multiply_convert_fusion.6, bf16[2048,64]{0,1:T(8,128)(2,1)S(1)} %copy-done.31), kind=kOutput, calls=%fused_computation.3 | convolution fusion | flops 1090519040 | bytes 51118080 | tf_op jit(solution)/shard_map/te,de->td/dot_general | solution.py:18
  534.9 95.9 %reduce-scatter.5.cloned.1.call-done = bf16[512,2048]{1,0:T(8,128)(2,1)} async-done(((bf16[4096,2048]{1,0:T(8,128)(2,1)}), bf16[512,2048]{1,0:T(8,128)(2,1)}) %reduce-scatter.5.cloned.1.call-update) | async-done | bytes 2097168 | tf_op jit(solution)/shard_map/reduce_scatter | solution.py:214
  630.9 7.1 add_convert_fusion.3
  638.2 29.4 %bitcast_convert_fusion = bf16[8,512,2048]{2,1,0:T(8,128)(2,1)} fusion(bf16[8,352,2048]{2,1,0:T(8,128)(2,1)} %param.32, bf16[8,8,72,352]{3,2,0,1:T(8,128)(2,1)} %get-tuple-element.136, pred[8,8,72,512]{3,2,1,0:T(8,128)(4,1)} %iota_compare_fusion.13), kind=kOutput, calls=%fused_computation.4 | convolution fusion | flops 16325279744 | bytes 33914880 | tf_op jit(solution)/shard_map/bect,becd->btd/dot_general | solution.py:18
  667.7 10.2 convolution_convert_fusion.11
  677.9 46.8 %all-reduce.8.cloned.1.call-done = bf16[512,2048]{1,0:T(8,128)(2,1)} async-done(((bf16[512,2048]{1,0:T(8,128)(2,1)}), bf16[512,2048]{1,0:T(8,128)(2,1)}) %all-reduce.8.cloned.1.call-update) | async-done | bytes 2097168 | tf_op jit(solution)/shard_map/psum | solution.py:215
  735.0 19.7 %fusion.69 = bf16[2560,4,128]{0,2,1:T(8,128)(2,1)} fusion(bf16[512,4,128]{0,2,1:T(8,128)(2,1)} %bitcast.252, f32[4,512]{1,0:T(4,128)S(1)} %copy-done.48, f32[4,512,2560]{2,1,0:T(8,128)} %fusion.3), kind=kOutput, calls=%fused_computation.106 | convolution fusion | flops 1359221248 | bytes 24125440 | tf_op jit(solution)/shard_map/hqk,qhd->khd/dot_general | solution.py:18
  754.7 15.2 %multiply_reduce_fusion = (f32[4,512]{1,0:T(4,128)S(1)}, f32[4,512,2560]{2,1,0:T(8,128)}) fusion(f32[4,512,2560]{2,1,0:T(8,128)} %get-tuple-element.145, f32[4,512]{1,0:T(4,128)S(1)} %copy-done.48, bf16[512,4,128]{0,2,1:T(8,128)(2,1)} %bitcast.253, bf16[2560,4,256]{0,2,1:T(8,128)(2,1)} %bitcast.239), kind=kOutput, calls=%fused_computation.9 | convolution fusion | flops 1357903872 | bytes 45105152 | tf_op jit(solution)/shard_map/qhd,khd->hqk/dot_general | solution.py:18
  769.9 14.6 %multiply_convert_fusion = bf16[4,512,2560]{2,1,0:T(8,128)(2,1)S(1)} fusion(f32[4,512,2560]{2,1,0:T(8,128)} %get-tuple-element.150, f32[4,512]{1,0:T(4,128)S(1)} %get-tuple-element.149, f32[4,512,2560]{2,1,0:T(8,128)} %get-tuple-element.145, f32[4,512]{1,0:T(4,128)S(1)} %copy-done.48), kind=kLoop, calls=%fused_computation.8 | loop fusion | flops 20971520 | bytes 52445184 | tf_op jit(solution)/shard_map/convert_element_type | solution.py:232
  843.4 7.2 fusion.92
  864.7 178.7 %all-reduce.10.cloned.1.call-done = (bf16[512,2048]{1,0:T(8,128)(2,1)}, bf16[512,2048]{1,0:T(8,128)(2,1)}, bf16[512,576]{0,1:T(8,128)(2,1)}, bf16[2048,64]{0,1:T(8,128)(2,1)}) async-done(((bf16[512,2048]{1,0:T(8,128)(2,1)}, bf16[512,2048]{1,0:T(8,128)(2,1)}, bf16[512,576]{0,1:T(8,128)(2,1)}, bf16[2048,64]{0,1:T(8,128)(2,1)}), (bf16[512,2048]{1,0:T(8,128)(2,1)}, bf16[512,2048]{1,0:T(8,128)(2,1)}, ...) | async-done | bytes 5046288 | tf_op jit(solution)/shard_map/psum | solution.py:272
  1059.2 40.1 %concatenate.47 = bf16[2048,2179]{0,1:T(8,128)(2,1)} concatenate(bf16[2048,512]{0,1:T(8,128)(2,1)} %convolution_convert_fusion.8, bf16[2048,768]{0,1:T(8,128)(2,1)} %convolution_convert_fusion.3, bf16[2048,576]{0,1:T(8,128)(2,1)} %convolution_convert_fusion.7, bf16[2048,256]{0,1:T(8,128)(2,1)} %copy.126, bf16[2048,64]{0,1:T(8,128)(2,1)S(1)} %copy-done.39, ...), dimensions={1} | concatenate | bytes 17850368 | tf_op jit(solution)/shard_map/concatenate | solution.py:66
  1101.9 21.4 %convolution_bitcast_fusion = f32[8,2048,352]{1,2,0:T(8,128)} fusion(bf16[8,8,72,2048]{3,2,1,0:T(8,128)(2,1)} %convolution_convert_fusion.1, bf16[8,8,72,352]{3,2,0,1:T(8,128)(2,1)} %get-tuple-element.114), kind=kOutput, calls=%fused_computation.53 | convolution fusion | flops 6643777536 | bytes 45187072 | tf_op jit(solution)/shard_map/becd,becf->edf/dot_general | solution.py:18
  1123.3 22.3 %convolution_bitcast_fusion.1 = f32[8,2048,352]{1,2,0:T(8,128)} fusion(bf16[8,8,72,2048]{3,2,1,0:T(8,128)(2,1)} %convolution_convert_fusion.1, bf16[8,8,72,352]{3,2,0,1:T(8,128)(2,1)S(1)} %copy-done.8), kind=kOutput, calls=%fused_computation.54 | convolution fusion | flops 6643777536 | bytes 45187072 | tf_op jit(solution)/shard_map/becd,becf->edf/dot_general | solution.py:18
  1145.6 18.2 %fusion.35 = f32[8,352,2048]{2,1,0:T(8,128)} fusion(bf16[8,8,72,352]{3,2,0,1:T(8,128)(2,1)} %get-tuple-element.136, bf16[8,8,72,2048]{3,2,1,0:T(8,128)(2,1)} %convolution_convert_fusion), kind=kOutput, calls=%fused_computation.52 | convolution fusion | flops 6643777536 | bytes 45187072 | tf_op jit(solution)/shard_map/becf,becd->efd/dot_general | solution.py:18
  1163.7 8.7 fusion.66
  (299 shorter events, 202.8 us)
Async XLA Ops:
  8.0 28.3 %copy-start = (bf16[2048,768]{1,0:T(8,128)(2,1)S(1)}, bf16[2048,768]{1,0:T(8,128)(2,1)}, u32[]{:S(2)}) copy-start(bf16[2048,768]{1,0:T(8,128)(2,1)} %param.23) | copy-start | bytes 9437188
  8.0 224.8 %all-reduce.6.cloned.1.call-start = ((), (), s32[]{:S(2)}) async-start(), calls=%async_computation.4 | async-start | bytes 4194304 | tf_op jit(solution)/shard_map/psum | solution.py:147
  20.9 44.2 %collective-permute-start = (bf16[512,576]{0,1:T(8,128)(2,1)}, bf16[512,576]{0,1:T(8,128)(2,1)}, u32[]{:S(2)}, u32[]{:S(2)}) collective-permute-start(bf16[512,576]{0,1:T(8,128)(2,1)} %pad_maximum_fusion.4), channel_id=1, source_target_pairs={{0,16},{4,20},{8,24},{12,28},{1,17},{5,21},{9,25},{13,29},{2,18},{... | collective-permute-start | bytes 1769480 | tf_op jit(solution)/shard_map/ppermute | solution.py:24
  26.6 39.6 %collective-permute-start.1 = (bf16[512,576]{0,1:T(8,128)(2,1)}, bf16[512,576]{0,1:T(8,128)(2,1)}, u32[]{:S(2)}, u32[]{:S(2)}) collective-permute-start(bf16[512,576]{0,1:T(8,128)(2,1)} %pad_maximum_fusion.4), channel_id=1, source_target_pairs={{0,12},{4,16},{8,20},{12,24},{16,28},{1,13},{5,17},{9,21},{13,25},... | collective-permute-start | bytes 1769480 | tf_op jit(solution)/shard_map/ppermute | solution.py:24
  29.9 37.3 %collective-permute-start.2 = (bf16[512,576]{0,1:T(8,128)(2,1)}, bf16[512,576]{0,1:T(8,128)(2,1)}, u32[]{:S(2)}, u32[]{:S(2)}) collective-permute-start(bf16[512,576]{0,1:T(8,128)(2,1)} %pad_maximum_fusion.4), channel_id=1, source_target_pairs={{0,8},{4,12},{8,16},{12,20},{16,24},{20,28},{1,9},{5,13},{9,17},{1... | collective-permute-start | bytes 1769480 | tf_op jit(solution)/shard_map/ppermute | solution.py:24
  32.9 35.5 %collective-permute-start.3 = (bf16[512,576]{0,1:T(8,128)(2,1)}, bf16[512,576]{0,1:T(8,128)(2,1)}, u32[]{:S(2)}, u32[]{:S(2)}) collective-permute-start(bf16[512,576]{0,1:T(8,128)(2,1)} %pad_maximum_fusion.4), channel_id=1, source_target_pairs={{0,4},{4,8},{8,12},{12,16},{16,20},{20,24},{24,28},{1,5},{5,9},{9,... | collective-permute-start | bytes 1769480 | tf_op jit(solution)/shard_map/ppermute | solution.py:24
  39.8 33.2 %copy-start.22 = (f32[512,768]{0,1:T(8,128)}, f32[512,768]{0,1:T(8,128)S(1)}, u32[]{:S(2)}) copy-start(f32[512,768]{0,1:T(8,128)S(1)} %fusion.159) | copy-start | bytes 4718596
  39.8 29.7 %copy-start.21 = (bf16[512,512]{0,1:T(8,128)(2,1)S(1)}, bf16[512,512]{0,1:T(8,128)(2,1)}, u32[]{:S(2)}) copy-start(bf16[512,512]{0,1:T(8,128)(2,1)} %copy-done.20) | copy-start | bytes 1572868
  39.8 29.7 %copy-start.69 = (bf16[512,1024]{1,0:T(8,128)(2,1)S(1)}, bf16[512,1024]{1,0:T(8,128)(2,1)}, u32[]{:S(2)}) copy-start(bf16[512,1024]{1,0:T(8,128)(2,1)} %param.26) | copy-start | bytes 3145732
  39.9 42.0 %copy-start.27 = (bf16[512,4,32]{0,2,1:T(8,128)(2,1)}, bf16[512,4,32]{0,2,1:T(8,128)(2,1)S(1)}, u32[]{:S(2)}) copy-start(bf16[512,4,32]{0,2,1:T(8,128)(2,1)S(1)} %get-tuple-element.125) | copy-start | bytes 393220
  40.0 42.0 %copy-start.29 = (bf16[512,4,32]{0,2,1:T(8,128)(2,1)}, bf16[512,4,32]{0,2,1:T(8,128)(2,1)S(1)}, u32[]{:S(2)}) copy-start(bf16[512,4,32]{0,2,1:T(8,128)(2,1)S(1)} %get-tuple-element.126) | copy-start | bytes 393220
  140.8 96.3 %copy-start.41 = (f32[2048]{0:T(1024)S(1)}, f32[2048]{0:T(1024)}, u32[]{:S(2)}) copy-start(f32[2048]{0:T(1024)} %param.28) | copy-start | bytes 24580
  140.9 111.8 %all-gather.5.cloned.1.call-start = ((), (), s32[]{:S(2)}) async-start(), calls=%async_computation.6 | async-start | bytes 18874368 | tf_op jit(solution)/shard_map/all_gather | solution.py:103
  141.4 189.2 %all-gather.3.cloned.1.call-start = ((), (), s32[]{:S(2)}) async-start(), calls=%async_computation.5 | async-start | bytes 18874368 | tf_op jit(solution)/shard_map/all_gather | solution.py:152
  239.6 391.3 %reduce-scatter.5.cloned.1.call-start = ((), (), s32[]{:S(2)}) async-start(), calls=%async_computation.7 | async-start | bytes 18874368 | tf_op jit(solution)/shard_map/reduce_scatter | solution.py:214
  514.9 209.8 %all-reduce.8.cloned.1.call-start = ((), (), s32[]{:S(2)}) async-start(), calls=%async_computation.9 | async-start | bytes 4194304 | tf_op jit(solution)/shard_map/psum | solution.py:215
  638.0 188.3 %reduce-scatter.7.cloned.1.call-start = ((), (), s32[]{:S(2)}) async-start(), calls=%async_computation.8 | async-start | bytes 18874368 | tf_op jit(solution)/shard_map/reduce_scatter | solution.py:218
  667.6 57.1 %copy-start.42 = (f32[2048]{0:T(1024)S(1)}, f32[2048]{0:T(1024)}, u32[]{:S(2)}) copy-start(f32[2048]{0:T(1024)} %param.28) | copy-start | bytes 24580
  667.6 57.1 %copy-start.44 = (f32[512]{0:T(512)S(1)}, f32[512]{0:T(512)}, u32[]{:S(2)}) copy-start(f32[512]{0:T(512)} %copy-done.43) | copy-start | bytes 6148
  667.6 375.7 %all-reduce.10.cloned.1.call-start = ((), (), s32[]{:S(2)}) async-start(), calls=%async_computation.12 | async-start | bytes 10092544 | tf_op jit(solution)/shard_map/psum | solution.py:272
  677.9 51.7 %copy-start.57 = (f32[512]{0:T(512)S(1)}, f32[512]{0:T(512)}, u32[]{:S(2)}) copy-start(f32[512]{0:T(512)} %copy-done.56) | copy-start | bytes 6148
  802.5 21.2 %collective-permute-start.4 = (bf16[512,576]{0,1:T(8,128)(2,1)}, bf16[512,576]{0,1:T(8,128)(2,1)S(1)}, u32[]{:S(2)}, u32[]{:S(2)}) collective-permute-start(bf16[512,576]{0,1:T(8,128)(2,1)} %get-tuple-element.118), channel_id=1, source_target_pairs={{16,0},{20,4},{24,8},{28,12},{17,1},{21,5},{25,9},{29,13},{18,2},{... | collective-permute-start | bytes 1769480 | tf_op jit(solution)/shard_map/ppermute | solution.py:24
  803.8 19.9 %collective-permute-start.5 = (bf16[512,576]{0,1:T(8,128)(2,1)}, bf16[512,576]{0,1:T(8,128)(2,1)S(1)}, u32[]{:S(2)}, u32[]{:S(2)}) collective-permute-start(bf16[512,576]{0,1:T(8,128)(2,1)} %get-tuple-element.121), channel_id=1, source_target_pairs={{12,0},{16,4},{20,8},{24,12},{28,16},{13,1},{17,5},{21,9},{25,13},... | collective-permute-start | bytes 1769480 | tf_op jit(solution)/shard_map/ppermute | solution.py:24
  805.1 18.6 %collective-permute-start.6 = (bf16[512,576]{0,1:T(8,128)(2,1)}, bf16[512,576]{0,1:T(8,128)(2,1)}, u32[]{:S(2)}, u32[]{:S(2)}) collective-permute-start(bf16[512,576]{0,1:T(8,128)(2,1)} %get-tuple-element.120), channel_id=1, source_target_pairs={{8,0},{12,4},{16,8},{20,12},{24,16},{28,20},{9,1},{13,5},{17,9},{2... | collective-permute-start | bytes 1769480 | tf_op jit(solution)/shard_map/ppermute | solution.py:24
  806.4 17.3 %collective-permute-start.7 = (bf16[512,576]{0,1:T(8,128)(2,1)S(1)}, bf16[512,576]{0,1:T(8,128)(2,1)}, u32[]{:S(2)}, u32[]{:S(2)}) collective-permute-start(bf16[512,576]{0,1:T(8,128)(2,1)S(1)} %get-tuple-element.119), channel_id=1, source_target_pairs={{4,0},{8,4},{12,8},{16,12},{20,16},{24,20},{28,24},{5,1},{9,5},{13... | collective-permute-start | bytes 1769480 | tf_op jit(solution)/shard_map/ppermute | solution.py:24
  832.1 267.1 %reduce-scatter.11.cloned.1.call-start = ((), (), s32[]{:S(2)}) async-start(), calls=%async_computation.11 | async-start | bytes 9732096 | tf_op jit(solution)/shard_map/reduce_scatter | solution.py:67
  843.4 329.7 %reduce-scatter.9.cloned.1.call-start = ((), (), s32[]{:S(2)}) async-start(), calls=%async_computation.10 | async-start | bytes 10063872 | tf_op jit(solution)/shard_map/reduce_scatter | solution.py:67
  861.2 183.5 %copy-start.46 = (f32[512]{0:T(512)S(1)}, f32[512]{0:T(512)}, u32[]{:S(2)}) copy-start(f32[512]{0:T(512)} %copy-done.45) | copy-start | bytes 6148
  861.2 183.5 %copy-start.59 = (f32[512]{0:T(512)S(1)}, f32[512]{0:T(512)}, u32[]{:S(2)}) copy-start(f32[512]{0:T(512)} %param.25) | copy-start | bytes 6148
  861.2 185.6 %copy-start.55 = (f32[512]{0:T(512)S(1)}, f32[512]{0:T(512)}, u32[]{:S(2)}) copy-start(f32[512]{0:T(512)} %copy-done.54) | copy-start | bytes 6148
  861.2 185.6 %copy-start.51 = (f32[512]{0:T(512)S(1)}, f32[512]{0:T(512)}, u32[]{:S(2)}) copy-start(f32[512]{0:T(512)} %copy-done.50) | copy-start | bytes 6148
  861.2 185.6 %copy-start.66 = (f32[32]{0:T(128)S(1)}, f32[32]{0:T(128)}, u32[]{:S(2)}) copy-start(f32[32]{0:T(128)} %copy-done.65) | copy-start | bytes 388
  (66 other events, 466.5 us)
Sparse Core Ops, SparseCore 0:
  141.0 91.8 all-reduce.5
  638.1 86.5 all-reduce.7
  832.3 211.0 all-reduce.9
Sparse Core Ops, SparseCore 1:
  143.4 95.0 all-gather.4
  240.9 89.7 all-gather.2
  515.0 115.8 reduce-scatter.4
  667.7 115.8 reduce-scatter.6
  843.5 99.9 reduce-scatter.10
  1099.3 73.7 reduce-scatter.8
where the time goes:
time: 1200 us
  waiting for transfers between devices  498 us (42%)
  matrix products  471 us (39%)
  other arithmetic  111 us (9%)
  local copies, waits for them, and re-layouts  67.1 us (6%)
  starting transfers between devices  20.8 us (2%)
  between operations  16.7 us (1%)
    dot_general x38, matrix products, dot(): return jnp.einsum(eq, a, b, preferred_element_type=F32)  433 us
    psum x1, waiting for transfers between devices, shards(): lax.psum((routed_block.astype(F32) + shared_result).astype(BF), 'tensor')  179 us
    reduce_scatter x1, waiting for transfers between devices, shards(): lax.psum_scatter(mid_part.astype(BF), 'dp', scatter_dimension=0, tiled=True)  95.9 us
    psum x1, waiting for transfers between devices, shards(): lax.psum(jnp.dot(attended, w_out, preferred_element_type=F32).astype(BF),...  91.4 us
    all_gather x1, waiting for transfers between devices, shards(): hidden_all = lax.all_gather(hidden_mid, 'dp', tiled=True)  59.2 us
    psum x1, waiting for transfers between devices, shards(): lax.psum((mid_block.astype(F32) + mid_from_shared).astype(BF), 'tensor')  46.8 us
    concatenate x1, local copies, waits for them, and re-layouts, scatter_sum(): joined = jnp.concatenate(parts, axis=1)  40.1 us
    ppermute x8, waiting for transfers between devices, passed_along(): return lax.ppermute(shard, axis, pairs)  25.1 us
  transfers between devices with their start and end apart: 17, of which 7 were waited for; matrix products, arithmetic and copies ran while one was open for 29% of the time, Pallas kernels for 0%

commit v1 on v0

--- a/solution.py
+++ b/solution.py
@@ -101,7 +101,6 @@
     window = (reach + 1) * tok_rows
     scale = (DN + DR) ** (-0.5)
     cot_all = lax.all_gather(cotangent, "dp", tiled=True)
-    route_all = lax.all_gather(route_ids, "dp", tiled=True)
     index_here = rank_dp * tok_rows + jnp.arange(tok_rows, dtype=jnp.int32)
     seq_here = lax.dynamic_slice_in_dim(seq_ids, rank_dp * tok_rows, tok_rows, 0)
     cosine, sine = rope_tables(seq_ids, seq_here, index_here)
@@ -149,7 +148,11 @@
     ).astype(F32)
     middle = token_features + attention
     hidden_mid = normed(middle, middle_gain).astype(BF)
-    hidden_all = lax.all_gather(hidden_mid, "dp", tiled=True)
+    route_all, hidden_all = jnp.split(
+        lax.all_gather(jnp.concatenate([route_ids, hidden_mid], axis=1), "dp", tiled=True),
+        [route_ids.shape[1]],
+        axis=1,
+    )
     shared_gate_val = jnp.dot(hidden_mid, shared_gate, preferred_element_type=F32)
     shared_up_val = jnp.dot(hidden_mid, shared_up, preferred_element_type=F32)
     shared_active = silu_gate(shared_gate_val, shared_up_val).astype(BF)

time: 1200 us -> 1310 us (1.092)
  waiting for transfers between devices: 498 us -> 584 us
  local copies, waits for them, and re-layouts: 67.1 us -> 90 us
    all_gather x1, waiting for transfers between devices: 59.2 us -> 92.2 us  [shards(): lax.all_gather(jnp.concatenate([route_ids, hidden_mid], axis=1), 'dp', ti...]
    reduce_scatter x1, waiting for transfers between devices: 0.01 us -> 27.5 us  [shards(): lax.psum_scatter(routed_part, 'dp', scatter_dimension=0, tiled=True)]
    reduce_scatter x2, waiting for transfers between devices: 0.62 us -> 26.3 us  [scatter_sum(): summed = lax.psum_scatter(joined, 'dp', scatter_dimension=0, tiled=True)]
    split x0 -> x3, local copies, waits for them, and re-layouts: none -> 22.3 us  [shards(): jnp.split(lax.all_gather(jnp.concatenate([route_ids, hidden_mid], axis=1)...]
    psum x1, waiting for transfers between devices: 179 us -> 162 us  [shards(): lax.psum((routed_block.astype(F32) + shared_result).astype(BF), 'tensor')]
  transfers between devices with their start and end apart: 17 -> 17, of which waited for: 7 -> 12; matrix products, arithmetic and copies ran while one was open for 29% -> 32% of each run, Pallas kernels for 0% -> 0%
where the time goes in v1:
time: 1310 us; the launch traced here: 1300 us
  waiting for transfers between devices  584 us (45%)
  matrix products  478 us (36%)
  other arithmetic  117 us (9%)
  local copies, waits for them, and re-layouts  90 us (7%)
  starting transfers between devices  20.8 us (2%)
  between operations  15.5 us (1%)
    dot_general x38, matrix products, dot(): return jnp.einsum(eq, a, b, preferred_element_type=F32)  441 us
    psum x1, waiting for transfers between devices, shards(): lax.psum((routed_block.astype(F32) + shared_result).astype(BF), 'tensor')  162 us
    reduce_scatter x1, waiting for transfers between devices, shards(): lax.psum_scatter(mid_part.astype(BF), 'dp', scatter_dimension=0, tiled=True)  98.1 us
    all_gather x1, waiting for transfers between devices, shards(): lax.all_gather(jnp.concatenate([route_ids, hidden_mid], axis=1), 'dp', ti...  92.2 us
    psum x1, waiting for transfers between devices, shards(): lax.psum(jnp.dot(attended, w_out, preferred_element_type=F32).astype(BF),...  91.8 us
    psum x1, waiting for transfers between devices, shards(): lax.psum((mid_block.astype(F32) + mid_from_shared).astype(BF), 'tensor')  44.6 us
    concatenate x1, local copies, waits for them, and re-layouts, scatter_sum(): joined = jnp.concatenate(parts, axis=1)  40.6 us
    ppermute x8, waiting for transfers between devices, passed_along(): return lax.ppermute(shard, axis, pairs)  35.3 us
  transfers between devices with their start and end apart: 17, of which 12 were waited for; matrix products, arithmetic and copies ran while one was open for 32% of the time, Pallas kernels for 0%

profile of v1, /device:TPU:0, one launch (start us, length us, event | category | flops | bytes accessed | tf_op | source)
XLA Modules:
  0.0 1304.8 jit_solution(4881146913539556140)
XLA Ops:
  39.1 25.1 %collective-permute-done = bf16[512,576]{0,1:T(8,128)(2,1)} collective-permute-done((bf16[512,576]{0,1:T(8,128)(2,1)}, bf16[512,576]{0,1:T(8,128)(2,1)}, u32[]{:S(2)}, u32[]{:S(2)}) %collective-permute-start) | collective-permute-done | bytes 589856 | tf_op jit(solution)/shard_map/ppermute | solution.py:24
  72.3 8.9 fusion.82
  81.2 13.6 %fusion.3 = f32[4,512,2560]{2,1,0:T(8,128)} fusion(f32[4,512,2560]{2,1,0:T(8,128)} %fusion.82, pred[512,2560]{1,0:T(8,128)(4,1)S(1)} %compare_and_fusion, bf16[2560,576]{0,1:T(8,128)(2,1)} %copy-done.37, bf16[512,4,32]{0,2,1:T(8,128)(2,1)S(1)} %get-tuple-element.126, bf16[512,4,32]{0,2,1:T(8,128)(2,1)S(1)} %get-tuple-element.125), kind=kOutput, calls=%fused_computation.7 | convolution fusion | flops 687341568 | bytes 43843584 | tf_op jit(solution)/shard_map/qhd,kd->hqk/dot_general | solution.py:18
  94.8 23.5 %fusion.172 = (f32[4,512]{1,0:T(4,128)S(1)}, f32[4,512,2560]{2,1,0:T(8,128)}) fusion(f32[4,512,2560]{2,1,0:T(8,128)} %fusion.3), kind=kOutput, calls=%fused_computation.255 | output fusion | flops 10488319 | bytes 41951232 | tf_op jit(solution)/shard_map/sub | solution.py:141
  118.3 17.4 %fusion.105 = bf16[4,128,512]{2,1,0:T(8,128)(2,1)} fusion(bf16[2560,4,256]{0,2,1:T(8,128)(2,1)} %bitcast.234, f32[4,512]{1,0:T(4,128)S(1)} %get-tuple-element.144, f32[4,512,2560]{2,1,0:T(8,128)} %fusion.3), kind=kOutput, calls=%fused_computation.148 | convolution fusion | flops 1358172672 | bytes 45096960 | tf_op jit(solution)/shard_map/hqk,khd->qhd/dot_general | solution.py:18
  140.4 91.8 %all-reduce.6.cloned.1.call-done = bf16[512,2048]{1,0:T(8,128)(2,1)} async-done(((bf16[512,2048]{1,0:T(8,128)(2,1)}), bf16[512,2048]{1,0:T(8,128)(2,1)}) %all-reduce.6.cloned.1.call-update) | async-done | bytes 2097168 | tf_op jit(solution)/shard_map/psum | solution.py:146
  242.0 92.2 %all-gather.3.cloned.1.call-done = bf16[4096,2054]{1,0:T(8,128)(2,1)} async-done(((bf16[512,2054]{1,0:T(8,128)(2,1)}), bf16[4096,2054]{1,0:T(8,128)(2,1)}) %all-gather.3.cloned.1.call-update) | async-done | bytes 16826384 | tf_op jit(solution)/shard_map/all_gather | solution.py:152
  338.1 18.5 %split.9 = bf16[4096,2048]{1,0:T(8,128)(2,1)} slice(bf16[4096,2054]{1,0:T(8,128)(2,1)} %all-gather.3.cloned.1.call-done), slice={[0:4096], [6:2054]} | slice | bytes 33554432 | tf_op jit(solution)/shard_map/split | solution.py:151
  360.2 20.3 %convolution_convert_fusion.1 = bf16[8,8,72,2048]{3,2,1,0:T(8,128)(2,1)} fusion(bf16[8,512,2048,1]{2,1,3,0:T(8,128)(2,1)} %bitcast.223, s32[8,8,512]{2,1,0:T(8,128)S(1)} %fusion.120), kind=kOutput, calls=%fused_computation.27 | convolution fusion | flops 9675472896 | bytes 35782656 | tf_op jit(solution)/shard_map/bect,btd->becd/dot_general | solution.py:18
  380.5 20.2 %fusion.18 = f32[8,8,72,352]{3,2,1,0:T(8,128)} fusion(bf16[8,8,72,2048]{3,2,1,0:T(8,128)(2,1)} %convolution_convert_fusion.1, bf16[8,2048,352]{1,2,0:T(8,128)(2,1)} %param.31), kind=kOutput, calls=%fused_computation.22 | convolution fusion | flops 6643777536 | bytes 36896768 | tf_op jit(solution)/shard_map/becd,edf->becf/dot_general | solution.py:18
  400.7 20.5 %fusion.20 = f32[8,8,72,352]{3,2,1,0:T(8,128)} fusion(bf16[8,8,72,2048]{3,2,1,0:T(8,128)(2,1)} %convolution_convert_fusion.1, bf16[8,2048,352]{1,2,0:T(8,128)(2,1)} %param.30), kind=kOutput, calls=%fused_computation.24 | convolution fusion | flops 6643777536 | bytes 36896768 | tf_op jit(solution)/shard_map/becd,edf->becf/dot_general | solution.py:18
  426.2 18.7 %convolution_convert_fusion = bf16[8,8,72,2048]{3,2,1,0:T(8,128)(2,1)} fusion(bf16[8,512,2048,1]{2,1,3,0:T(8,128)(2,1)} %bitcast.245, s32[8,8,512]{2,1,0:T(8,128)S(1)} %fusion.120), kind=kOutput, calls=%fused_computation.26 | convolution fusion | flops 9675472896 | bytes 35782656 | tf_op jit(solution)/shard_map/bect,btd->becd/dot_general | solution.py:18
  444.9 24.3 %fusion.39 = (bf16[8,8,72]{2,0,1:T(8,128)(2,1)S(1)}, bf16[8,8,72,352]{3,2,0,1:T(8,128)(2,1)}, f32[8,8,72,352]{3,2,1,0:T(8,128)}) fusion(f32[8,8,72,352]{3,2,1,0:T(8,128)} %fusion.18, f32[8,8,72,352]{3,2,1,0:T(8,128)} %fusion.20, bf16[8,352,2048]{2,1,0:T(8,128)(2,1)} %param.32, bf16[8,8,72,2048]{3,2,1,0:T(8,128)(2,1)} %convolution_convert_fusion), kind=kOutput, calls=%fused_computation.56 | convolution fusion | flops 6658371072 | bytes 53126144 | tf_op jit(solution)/shard_map/becd,efd->becf/dot_general | solution.py:18
  470.8 10.2 fusion.173
  484.0 10.0 multiply_convert_fusion.1
  493.9 21.4 %fusion.31 = f32[8,8,72,2048]{3,2,0,1:T(8,128)} fusion(bf16[8,2048,352]{1,2,0:T(8,128)(2,1)} %param.30, bf16[8,8,72,352]{3,2,0,1:T(8,128)(2,1)} %get-tuple-element.115), kind=kOutput, calls=%fused_computation.33 | convolution fusion | flops 6643777536 | bytes 52527104 | tf_op jit(solution)/shard_map/becf,edf->becd/dot_general | solution.py:18
  515.4 40.0 %fusion.5 = f32[8,512,2048,1]{2,1,3,0:T(8,128)} fusion(f32[8,8,72,2048]{3,2,0,1:T(8,128)} %fusion.31, bf16[8,2048,352]{1,2,0:T(8,128)(2,1)} %param.31, bf16[8,8,72,352]{3,2,0,1:T(8,128)(2,1)} %get-tuple-element.114, pred[8,8,72,512]{3,2,1,0:T(8,128)(4,1)} %iota_compare_fusion.14), kind=kOutput, calls=%fused_computation.12 | convolution fusion | flops 16326328320 | bytes 88440832 | tf_op jit(solution)/shard_map/bect,becd->btd/dot_general | solution.py:18
  555.4 17.1 %fusion.1 = bf16[4096,2048]{1,0:T(8,128)(2,1)} fusion(f32[8,512,2048,1]{2,1,3,0:T(8,128)} %fusion.5, bf16[4096,64]{0,1:T(8,128)(2,1)} %multiply_convert_fusion.6, bf16[2048,64]{0,1:T(8,128)(2,1)S(1)} %copy-done.39), kind=kOutput, calls=%fused_computation.3 | convolution fusion | flops 1090519040 | bytes 51118080 | tf_op jit(solution)/shard_map/te,de->td/dot_general | solution.py:18
  590.6 98.1 %reduce-scatter.5.cloned.1.call-done = bf16[512,2048]{1,0:T(8,128)(2,1)} async-done(((bf16[4096,2048]{1,0:T(8,128)(2,1)}), bf16[512,2048]{1,0:T(8,128)(2,1)}) %reduce-scatter.5.cloned.1.call-update) | async-done | bytes 2097168 | tf_op jit(solution)/shard_map/reduce_scatter | solution.py:217
  696.0 29.4 %bitcast_convert_fusion = bf16[8,512,2048]{2,1,0:T(8,128)(2,1)} fusion(bf16[8,352,2048]{2,1,0:T(8,128)(2,1)} %param.32, bf16[8,8,72,352]{3,2,0,1:T(8,128)(2,1)} %get-tuple-element.136, pred[8,8,72,512]{3,2,1,0:T(8,128)(4,1)} %iota_compare_fusion.13), kind=kOutput, calls=%fused_computation.4 | convolution fusion | flops 16325279744 | bytes 33914880 | tf_op jit(solution)/shard_map/bect,becd->btd/dot_general | solution.py:18
  725.5 12.3 convolution_convert_fusion.11
  737.9 44.6 %all-reduce.8.cloned.1.call-done = bf16[512,2048]{1,0:T(8,128)(2,1)} async-done(((bf16[512,2048]{1,0:T(8,128)(2,1)}), bf16[512,2048]{1,0:T(8,128)(2,1)}) %all-reduce.8.cloned.1.call-update) | async-done | bytes 2097168 | tf_op jit(solution)/shard_map/psum | solution.py:218
  792.5 24.8 %fusion.69 = bf16[2560,4,128]{0,2,1:T(8,128)(2,1)} fusion(bf16[512,4,128]{0,2,1:T(8,128)(2,1)} %bitcast.248, f32[4,512]{1,0:T(4,128)S(1)} %copy-done.49, f32[4,512,2560]{2,1,0:T(8,128)} %fusion.3), kind=kOutput, calls=%fused_computation.106 | convolution fusion | flops 1359221248 | bytes 24125440 | tf_op jit(solution)/shard_map/hqk,qhd->khd/dot_general | solution.py:18
  817.3 15.4 %multiply_reduce_fusion = (f32[4,512]{1,0:T(4,128)S(1)}, f32[4,512,2560]{2,1,0:T(8,128)}) fusion(f32[4,512,2560]{2,1,0:T(8,128)} %get-tuple-element.145, f32[4,512]{1,0:T(4,128)S(1)} %copy-done.49, bf16[512,4,128]{0,2,1:T(8,128)(2,1)} %bitcast.249, bf16[2560,4,256]{0,2,1:T(8,128)(2,1)} %bitcast.235), kind=kOutput, calls=%fused_computation.9 | convolution fusion | flops 1357903872 | bytes 45105152 | tf_op jit(solution)/shard_map/qhd,khd->hqk/dot_general | solution.py:18
  832.7 15.4 %multiply_convert_fusion = bf16[4,512,2560]{2,1,0:T(8,128)(2,1)S(1)} fusion(f32[4,512,2560]{2,1,0:T(8,128)} %get-tuple-element.150, f32[4,512]{1,0:T(4,128)S(1)} %get-tuple-element.149, f32[4,512,2560]{2,1,0:T(8,128)} %get-tuple-element.145, f32[4,512]{1,0:T(4,128)S(1)} %copy-done.49), kind=kLoop, calls=%fused_computation.8 | loop fusion | flops 20971520 | bytes 52445184 | tf_op jit(solution)/shard_map/convert_element_type | solution.py:235
  900.3 27.5 %reduce-scatter.7.cloned.1.call-done = bf16[512,2048]{1,0:T(8,128)(2,1)} async-done(((bf16[4096,2048]{1,0:T(8,128)(2,1)}), bf16[512,2048]{1,0:T(8,128)(2,1)}) %reduce-scatter.7.cloned.1.call-update) | async-done | bytes 2097168 | tf_op jit(solution)/shard_map/reduce_scatter | solution.py:221
  966.3 162.2 %all-reduce.10.cloned.1.call-done = (bf16[512,2048]{1,0:T(8,128)(2,1)}, bf16[512,2048]{1,0:T(8,128)(2,1)}, bf16[512,576]{0,1:T(8,128)(2,1)}, bf16[2048,64]{0,1:T(8,128)(2,1)}) async-done(((bf16[512,2048]{1,0:T(8,128)(2,1)}, bf16[512,2048]{1,0:T(8,128)(2,1)}, bf16[512,576]{0,1:T(8,128)(2,1)}, bf16[2048,64]{0,1:T(8,128)(2,1)}), (bf16[512,2048]{1,0:T(8,128)(2,1)}, bf16[512,2048]{1,0:T(8,128)(2,1)}, ...) | async-done | bytes 5046288 | tf_op jit(solution)/shard_map/psum | solution.py:275
  1144.9 40.6 %concatenate.51 = bf16[2048,2179]{0,1:T(8,128)(2,1)} concatenate(bf16[2048,512]{0,1:T(8,128)(2,1)} %convolution_convert_fusion.8, bf16[2048,768]{0,1:T(8,128)(2,1)} %convolution_convert_fusion.3, bf16[2048,576]{0,1:T(8,128)(2,1)} %convolution_convert_fusion.7, bf16[2048,256]{0,1:T(8,128)(2,1)} %copy.130, bf16[2048,64]{0,1:T(8,128)(2,1)S(1)} %copy-done.40, ...), dimensions={1} | concatenate | bytes 17850368 | tf_op jit(solution)/shard_map/concatenate | solution.py:66
  1185.5 19.2 %reduce-scatter.11.cloned.1.call-done = bf16[256,2112]{0,1:T(8,128)(2,1)} async-done(((bf16[2048,2112]{0,1:T(8,128)(2,1)}), bf16[256,2112]{0,1:T(8,128)(2,1)}) %reduce-scatter.11.cloned.1.call-update) | async-done | bytes 1081360 | tf_op jit(solution)/shard_map/reduce_scatter | solution.py:67
  1207.3 20.0 %convolution_bitcast_fusion = f32[8,2048,352]{1,2,0:T(8,128)} fusion(bf16[8,8,72,2048]{3,2,1,0:T(8,128)(2,1)} %convolution_convert_fusion.1, bf16[8,8,72,352]{3,2,0,1:T(8,128)(2,1)} %get-tuple-element.114), kind=kOutput, calls=%fused_computation.53 | convolution fusion | flops 6643777536 | bytes 45187072 | tf_op jit(solution)/shard_map/becd,becf->edf/dot_general | solution.py:18
  1227.3 21.7 %convolution_bitcast_fusion.1 = f32[8,2048,352]{1,2,0:T(8,128)} fusion(bf16[8,8,72,2048]{3,2,1,0:T(8,128)(2,1)} %convolution_convert_fusion.1, bf16[8,8,72,352]{3,2,0,1:T(8,128)(2,1)S(1)} %copy-done.8), kind=kOutput, calls=%fused_computation.54 | convolution fusion | flops 6643777536 | bytes 45187072 | tf_op jit(solution)/shard_map/becd,becf->edf/dot_general | solution.py:18
  1249.0 18.4 %fusion.35 = f32[8,352,2048]{2,1,0:T(8,128)} fusion(bf16[8,8,72,352]{3,2,0,1:T(8,128)(2,1)} %get-tuple-element.136, bf16[8,8,72,2048]{3,2,1,0:T(8,128)(2,1)} %convolution_convert_fusion), kind=kOutput, calls=%fused_computation.52 | convolution fusion | flops 6643777536 | bytes 45187072 | tf_op jit(solution)/shard_map/becf,becd->efd/dot_general | solution.py:18
  (301 shorter events, 246.1 us)
Async XLA Ops:
  7.2 28.3 %copy-start = (bf16[2048,768]{1,0:T(8,128)(2,1)S(1)}, bf16[2048,768]{1,0:T(8,128)(2,1)}, u32[]{:S(2)}) copy-start(bf16[2048,768]{1,0:T(8,128)(2,1)} %param.23) | copy-start | bytes 9437188
  7.2 224.9 %all-reduce.6.cloned.1.call-start = ((), (), s32[]{:S(2)}) async-start(), calls=%async_computation.4 | async-start | bytes 4194304 | tf_op jit(solution)/shard_map/psum | solution.py:146
  20.1 44.2 %collective-permute-start = (bf16[512,576]{0,1:T(8,128)(2,1)}, bf16[512,576]{0,1:T(8,128)(2,1)}, u32[]{:S(2)}, u32[]{:S(2)}) collective-permute-start(bf16[512,576]{0,1:T(8,128)(2,1)} %pad_maximum_fusion.5), channel_id=1, source_target_pairs={{0,16},{4,20},{8,24},{12,28},{1,17},{5,21},{9,25},{13,29},{2,18},{... | collective-permute-start | bytes 1769480 | tf_op jit(solution)/shard_map/ppermute | solution.py:24
  25.8 39.6 %collective-permute-start.1 = (bf16[512,576]{0,1:T(8,128)(2,1)}, bf16[512,576]{0,1:T(8,128)(2,1)}, u32[]{:S(2)}, u32[]{:S(2)}) collective-permute-start(bf16[512,576]{0,1:T(8,128)(2,1)} %pad_maximum_fusion.5), channel_id=1, source_target_pairs={{0,12},{4,16},{8,20},{12,24},{16,28},{1,13},{5,17},{9,21},{13,25},... | collective-permute-start | bytes 1769480 | tf_op jit(solution)/shard_map/ppermute | solution.py:24
  29.1 37.3 %collective-permute-start.2 = (bf16[512,576]{0,1:T(8,128)(2,1)}, bf16[512,576]{0,1:T(8,128)(2,1)}, u32[]{:S(2)}, u32[]{:S(2)}) collective-permute-start(bf16[512,576]{0,1:T(8,128)(2,1)} %pad_maximum_fusion.5), channel_id=1, source_target_pairs={{0,8},{4,12},{8,16},{12,20},{16,24},{20,28},{1,9},{5,13},{9,17},{1... | collective-permute-start | bytes 1769480 | tf_op jit(solution)/shard_map/ppermute | solution.py:24
  32.1 35.5 %collective-permute-start.3 = (bf16[512,576]{0,1:T(8,128)(2,1)}, bf16[512,576]{0,1:T(8,128)(2,1)}, u32[]{:S(2)}, u32[]{:S(2)}) collective-permute-start(bf16[512,576]{0,1:T(8,128)(2,1)} %pad_maximum_fusion.5), channel_id=1, source_target_pairs={{0,4},{4,8},{8,12},{12,16},{16,20},{20,24},{24,28},{1,5},{5,9},{9,... | collective-permute-start | bytes 1769480 | tf_op jit(solution)/shard_map/ppermute | solution.py:24
  39.0 33.3 %copy-start.23 = (f32[512,768]{0,1:T(8,128)}, f32[512,768]{0,1:T(8,128)S(1)}, u32[]{:S(2)}) copy-start(f32[512,768]{0,1:T(8,128)S(1)} %fusion.159) | copy-start | bytes 4718596
  39.0 29.7 %copy-start.22 = (bf16[512,512]{0,1:T(8,128)(2,1)S(1)}, bf16[512,512]{0,1:T(8,128)(2,1)}, u32[]{:S(2)}) copy-start(bf16[512,512]{0,1:T(8,128)(2,1)} %copy-done.21) | copy-start | bytes 1572868
  39.0 29.7 %copy-start.70 = (bf16[512,1024]{1,0:T(8,128)(2,1)S(1)}, bf16[512,1024]{1,0:T(8,128)(2,1)}, u32[]{:S(2)}) copy-start(bf16[512,1024]{1,0:T(8,128)(2,1)} %param.26) | copy-start | bytes 3145732
  39.1 42.1 %copy-start.28 = (bf16[512,4,32]{0,2,1:T(8,128)(2,1)}, bf16[512,4,32]{0,2,1:T(8,128)(2,1)S(1)}, u32[]{:S(2)}) copy-start(bf16[512,4,32]{0,2,1:T(8,128)(2,1)S(1)} %get-tuple-element.125) | copy-start | bytes 393220
  39.1 42.1 %copy-start.30 = (bf16[512,4,32]{0,2,1:T(8,128)(2,1)}, bf16[512,4,32]{0,2,1:T(8,128)(2,1)S(1)}, u32[]{:S(2)}) copy-start(bf16[512,4,32]{0,2,1:T(8,128)(2,1)S(1)} %get-tuple-element.126) | copy-start | bytes 393220
  140.1 95.8 %copy-start.42 = (f32[2048]{0:T(1024)S(1)}, f32[2048]{0:T(1024)}, u32[]{:S(2)}) copy-start(f32[2048]{0:T(1024)} %param.28) | copy-start | bytes 24580
  140.1 194.1 %all-gather.3.cloned.1.call-start = ((), (), s32[]{:S(2)}) async-start(), calls=%async_computation.5 | async-start | bytes 20054016 | tf_op jit(solution)/shard_map/all_gather | solution.py:152
  240.8 185.3 %all-gather.5.cloned.1.call-start = ((), (), s32[]{:S(2)}) async-start(), calls=%async_computation.6 | async-start | bytes 18874368 | tf_op jit(solution)/shard_map/all_gather | solution.py:103
  241.6 447.1 %reduce-scatter.5.cloned.1.call-start = ((), (), s32[]{:S(2)}) async-start(), calls=%async_computation.7 | async-start | bytes 18874368 | tf_op jit(solution)/shard_map/reduce_scatter | solution.py:217
  572.5 209.9 %all-reduce.8.cloned.1.call-start = ((), (), s32[]{:S(2)}) async-start(), calls=%async_computation.9 | async-start | bytes 4194304 | tf_op jit(solution)/shard_map/psum | solution.py:218
  695.8 232.1 %reduce-scatter.7.cloned.1.call-start = ((), (), s32[]{:S(2)}) async-start(), calls=%async_computation.8 | async-start | bytes 18874368 | tf_op jit(solution)/shard_map/reduce_scatter | solution.py:221
  725.4 57.0 %copy-start.43 = (f32[2048]{0:T(1024)S(1)}, f32[2048]{0:T(1024)}, u32[]{:S(2)}) copy-start(f32[2048]{0:T(1024)} %param.28) | copy-start | bytes 24580
  725.4 57.0 %copy-start.45 = (f32[512]{0:T(512)S(1)}, f32[512]{0:T(512)}, u32[]{:S(2)}) copy-start(f32[512]{0:T(512)} %copy-done.44) | copy-start | bytes 6148
  725.5 403.1 %all-reduce.10.cloned.1.call-start = ((), (), s32[]{:S(2)}) async-start(), calls=%async_computation.12 | async-start | bytes 10092544 | tf_op jit(solution)/shard_map/psum | solution.py:275
  737.9 49.4 %copy-start.58 = (f32[512]{0:T(512)S(1)}, f32[512]{0:T(512)}, u32[]{:S(2)}) copy-start(f32[512]{0:T(512)} %copy-done.57) | copy-start | bytes 6148
  866.6 25.1 %collective-permute-start.4 = (bf16[512,576]{0,1:T(8,128)(2,1)}, bf16[512,576]{0,1:T(8,128)(2,1)S(1)}, u32[]{:S(2)}, u32[]{:S(2)}) collective-permute-start(bf16[512,576]{0,1:T(8,128)(2,1)} %get-tuple-element.118), channel_id=1, source_target_pairs={{16,0},{20,4},{24,8},{28,12},{17,1},{21,5},{25,9},{29,13},{18,2},{... | collective-permute-start | bytes 1769480 | tf_op jit(solution)/shard_map/ppermute | solution.py:24
  867.9 23.8 %collective-permute-start.5 = (bf16[512,576]{0,1:T(8,128)(2,1)}, bf16[512,576]{0,1:T(8,128)(2,1)S(1)}, u32[]{:S(2)}, u32[]{:S(2)}) collective-permute-start(bf16[512,576]{0,1:T(8,128)(2,1)} %get-tuple-element.121), channel_id=1, source_target_pairs={{12,0},{16,4},{20,8},{24,12},{28,16},{13,1},{17,5},{21,9},{25,13},... | collective-permute-start | bytes 1769480 | tf_op jit(solution)/shard_map/ppermute | solution.py:24
  869.2 28.6 %collective-permute-start.6 = (bf16[512,576]{0,1:T(8,128)(2,1)}, bf16[512,576]{0,1:T(8,128)(2,1)}, u32[]{:S(2)}, u32[]{:S(2)}) collective-permute-start(bf16[512,576]{0,1:T(8,128)(2,1)} %get-tuple-element.120), channel_id=1, source_target_pairs={{8,0},{12,4},{16,8},{20,12},{24,16},{28,20},{9,1},{13,5},{17,9},{2... | collective-permute-start | bytes 1769480 | tf_op jit(solution)/shard_map/ppermute | solution.py:24
  870.5 27.3 %collective-permute-start.7 = (bf16[512,576]{0,1:T(8,128)(2,1)S(1)}, bf16[512,576]{0,1:T(8,128)(2,1)}, u32[]{:S(2)}, u32[]{:S(2)}) collective-permute-start(bf16[512,576]{0,1:T(8,128)(2,1)S(1)} %get-tuple-element.119), channel_id=1, source_target_pairs={{4,0},{8,4},{12,8},{16,12},{20,16},{24,20},{28,24},{5,1},{9,5},{13... | collective-permute-start | bytes 1769480 | tf_op jit(solution)/shard_map/ppermute | solution.py:24
  933.7 271.0 %reduce-scatter.11.cloned.1.call-start = ((), (), s32[]{:S(2)}) async-start(), calls=%async_computation.11 | async-start | bytes 9732096 | tf_op jit(solution)/shard_map/reduce_scatter | solution.py:67
  945.0 338.3 %reduce-scatter.9.cloned.1.call-start = ((), (), s32[]{:S(2)}) async-start(), calls=%async_computation.10 | async-start | bytes 10063872 | tf_op jit(solution)/shard_map/reduce_scatter | solution.py:67
  962.8 167.1 %copy-start.47 = (f32[512]{0:T(512)S(1)}, f32[512]{0:T(512)}, u32[]{:S(2)}) copy-start(f32[512]{0:T(512)} %copy-done.46) | copy-start | bytes 6148
  962.8 167.1 %copy-start.60 = (f32[512]{0:T(512)S(1)}, f32[512]{0:T(512)}, u32[]{:S(2)}) copy-start(f32[512]{0:T(512)} %param.25) | copy-start | bytes 6148
  962.8 169.2 %copy-start.56 = (f32[512]{0:T(512)S(1)}, f32[512]{0:T(512)}, u32[]{:S(2)}) copy-start(f32[512]{0:T(512)} %copy-done.55) | copy-start | bytes 6148
  962.8 169.2 %copy-start.52 = (f32[512]{0:T(512)S(1)}, f32[512]{0:T(512)}, u32[]{:S(2)}) copy-start(f32[512]{0:T(512)} %copy-done.51) | copy-start | bytes 6148
  962.8 169.2 %copy-start.67 = (f32[32]{0:T(128)S(1)}, f32[32]{0:T(128)}, u32[]{:S(2)}) copy-start(f32[32]{0:T(128)} %copy-done.66) | copy-start | bytes 388
  (65 other events, 459.6 us)
Sparse Core Ops, SparseCore 0:
  140.2 91.8 all-reduce.5
  241.0 93.2 all-gather.2
  336.3 89.8 all-gather.4
  572.6 115.9 reduce-scatter.4
  695.9 86.4 all-reduce.7
  786.4 141.4 reduce-scatter.6
  933.8 194.6 all-reduce.9
  1133.0 71.5 reduce-scatter.10
  1208.3 74.8 reduce-scatter.8
